TPU v7x, 128 devices: a whole 4x4x4 slice. The times are simulated.
128 devices in a mesh: slab: 8 (over z, x_lo), view: 16 (over y, x_hi, core).
Axes of the slice: x: 4 (x_hi: 2, x_lo: 2; x = x_hi * 2 + x_lo), y: 4, z: 4, core: 2. Of those that a mesh axis runs over, the one named last changes fastest.
Arguments:
- volume: float32 [128, 32768], P(None, 'slab'), may hold values from 0 to 1
- measured: bfloat16 [32, 128, 2048], P('view'), may hold values from 0 to 8
- weights: bfloat16 [32, 32768, 1024], P('view', 'slab'), as said below
- offsets: int32 [32, 8], P('view', 'slab'), may hold values from 0 to 1024
- order: int32 [32], P('view'), may hold values from 0 to 1, as said below
Outputs:
- updated: float32 [128, 32768], P(None, 'slab')
- mismatch: float32 [32, 128, 2048], P('view')
Inputs may be any that keep to these rules, and one draw needn't show every extreme that they name: `order`: each aligned group of 2 entries is a permutation of 0 to 1. `weights`: every weight is zero or positive, and every voxel has a positive weight in every view.
All inputs are finite; a program needn't handle non-finite values.
Results may differ from a plain program's by a relative error of at most 0.00055.
Values sent between devices are 32-bit elements; how exact they have to be, the bound alone decides.
A program may use at most 128 MiB of HBM per device.

v0:
```python
import jax
import jax.numpy as jnp
from jax import lax
from jax.sharding import PartitionSpec as P

RELAXATION = 0.9


def in_blocks(array, dim, length):
    before, after = (array.shape[:dim], array.shape[dim + 1 :])
    return jnp.moveaxis(array.reshape(*before, length, -1, *after), dim, 0)


def sent_and_summed(array, axis, dim):
    tiles = in_blocks(array, dim, lax.axis_size(axis))
    arrived = lax.all_to_all(tiles, axis, split_axis=0, concat_axis=0, tiled=True)
    return arrived.sum(axis=0)


def sent_to_all(array, axis):
    length = lax.axis_size(axis)
    return lax.all_to_all(
        jnp.broadcast_to(array[None], (length, *array.shape)), axis, 0, 0, tiled=True
    )


def joined_along(tiles, dim):
    tiles = jnp.moveaxis(tiles, 0, dim)
    lengths = tiles.shape
    return tiles.reshape(*lengths[:dim], lengths[dim] * lengths[dim + 1], *lengths[dim + 2 :])


def collect(array, axis, dim):
    tiles = sent_to_all(array, axis)
    return joined_along(tiles, dim)


def per_device(volume, measured, weights, offsets, order):
    subsets = weights.shape[0]
    band_width = weights.shape[2]
    slice_rows = measured.shape[1]
    detector_cols = measured.shape[2]
    mismatch = jnp.zeros(measured.shape, jnp.float32)
    for subset_index in range(subsets):
        chosen_view = order[subset_index]
        footprint = lax.dynamic_index_in_dim(weights, chosen_view, 0, keepdims=False)
        first_column = offsets[chosen_view, 0]
        observed = lax.dynamic_index_in_dim(measured, chosen_view, 0, keepdims=False).astype(
            jnp.float32
        )
        partial_value = jnp.dot(
            volume.astype(jnp.bfloat16), footprint, preferred_element_type=jnp.float32
        )
        placed = lax.dynamic_update_slice(
            jnp.zeros((slice_rows, detector_cols), jnp.float32),
            partial_value,
            (jnp.int32(0), first_column),
        )
        placed_row = lax.dynamic_update_slice(
            jnp.zeros((detector_cols,), jnp.float32),
            jnp.sum(footprint, axis=0, dtype=jnp.float32),
            (first_column,),
        )
        projection_part, row_part = (
            sent_and_summed(placed, "slab", 1),
            sent_and_summed(placed_row, "slab", 0),
        )
        share_width = projection_part.shape[1]
        observed_part = lax.dynamic_slice_in_dim(
            observed, lax.axis_index("slab") * share_width, share_width, 1
        )
        correction_part = (observed_part - projection_part) / jnp.maximum(row_part, 1.0)
        correction = collect(correction_part, "slab", 1)
        mismatch = lax.dynamic_update_index_in_dim(mismatch, correction, chosen_view, 0)
        band_values = lax.dynamic_slice_in_dim(correction, first_column, band_width, 1).astype(
            jnp.bfloat16
        )
        back_terms = lax.dot_general(
            band_values, footprint, (((1,), (1,)), ((), ())), preferred_element_type=jnp.float32
        )
        col_total = jnp.sum(footprint, axis=1, dtype=jnp.float32)
        back_part, weight_part = (
            sent_and_summed(back_terms, "view", 1),
            sent_and_summed(col_total, "view", 0),
        )
        share_width = back_part.shape[1]
        volume_part = lax.dynamic_slice_in_dim(
            volume, lax.axis_index("view") * share_width, share_width, 1
        )
        new_part = volume_part + RELAXATION * back_part / weight_part[None, :]
        volume = lax.all_gather(new_part, "view", axis=1, tiled=True)
    return (volume, mismatch)


def solution(mesh):
    placed = (
        P(None, "slab"),
        P("view", None, None),
        P("view", "slab", None),
        P("view", "slab"),
        P("view"),
    )
    return jax.shard_map(
        per_device,
        mesh=mesh,
        in_specs=placed,
        out_specs=(P(None, "slab"), P("view", None, None)),
        check_vma=False,
    )
```

profile of v0, /device:TPU:1, one launch (start us, length us, event | category | flops | bytes accessed | tf_op | source)
XLA Modules:
  0.0 338.8 jit_solution(11723134778477959800)
XLA Ops:
  7.2 1.3 fusion.17
  12.4 1.4 constant_dynamic-slice_fusion
  15.0 13.8 %convert_reduce_fusion.2 = (f32[4096]{0:T(1024)}, f32[1024]{0:T(1024)S(1)}, bf16[1,4096,1024]{2,1,0:T(8,128)(2,1)}, f32[1024]{0:T(1024)S(1)}, f32[4096]{0:T(1024)}, /*index=5*/bf16[1,4096,1024]{2,1,0:T(8,128)(2,1)}) fusion(bf16[2,4096,1024]{2,1,0:T(8,128)(2,1)} %param.7, s32[]{:T(128)S(6)} %select_n.34, s32[]{:T(128)S(6)} %select_n.37), kind=kLoop, calls=%fused_computation.2 | loop fusion | flops 25155584 | bytes 33595400 | tf_op jit(solution)/shard_map/reduce_sum | solution.py:81
  30.0 1.4 dynamic_update_slice.20
  31.5 6.8 %all-to-all-start.1 = ((f32[8,1,256]{2,1,0:T(1,128)}), f32[8,1,256]{2,1,0:T(1,128)S(1)}, u32[]{:S(2)}, u32[]{:S(2)}) async-start(f32[8,1,256]{2,1,0:T(1,128)} %bitcast.7), calls=%async_computation.1 | async-start | bytes 16384 | tf_op jit(solution)/shard_map/all_to_all | solution.py:16
  38.3 5.7 %fusion.4 = f32[128,1024]{0,1:T(8,128)S(1)} fusion(bf16[1,4096,1024]{2,1,0:T(8,128)(2,1)} %get-tuple-element.7, f32[128,4096]{1,0:T(8,128)S(1)} %copy-done), kind=kOutput, calls=%fused_computation.10 | convolution fusion | flops 1074266112 | bytes 11010048 | tf_op jit(solution)/shard_map/dot_general | solution.py:51
  45.1 3.0 dynamic_update_slice.19
  48.0 5.1 %all-to-all-start = ((f32[8,128,256]{1,2,0:T(8,128)}), f32[8,128,256]{1,2,0:T(8,128)S(1)}, u32[]{:S(2)}, u32[]{:S(2)}) async-start(f32[8,128,256]{1,2,0:T(8,128)} %bitcast.6), calls=%async_computation | async-start | bytes 2097152 | tf_op jit(solution)/shard_map/all_to_all | solution.py:16
  54.1 13.0 %all-to-all-done = f32[8,128,256]{1,2,0:T(8,128)S(1)} async-done(((f32[8,128,256]{1,2,0:T(8,128)}), f32[8,128,256]{1,2,0:T(8,128)S(1)}, u32[]{:S(2)}, u32[]{:S(2)}) %all-to-all-start) | async-done | bytes 1048608 | tf_op jit(solution)/shard_map/all_to_all | solution.py:16
  67.5 18.1 %all_to_all.66 = f32[8,128,256]{2,1,0:T(8,128)S(1)} all-to-all(f32[8,128,256]{2,1,0:T(8,128)S(1)} %broadcast_in_dim.13), channel_id=1, replica_groups=mesh['slab'=8,'view'=16] {'slab'}, dimensions={0} | all-to-all | bytes 2097152 | tf_op jit(solution)/shard_map/all_to_all | solution.py:22
  85.6 9.1 %all-to-all-start.4 = ((f32[16,1,256]{2,1,0:T(1,128)}), f32[16,1,256]{2,1,0:T(1,128)S(1)}, u32[]{:S(2)}, u32[]{:S(2)}) async-start(f32[16,1,256]{2,1,0:T(1,128)} %bitcast.13), calls=%async_computation.4 | async-start | bytes 32768 | tf_op jit(solution)/shard_map/all_to_all | solution.py:16
  94.7 7.6 %convolution_bitcast_fusion.1 = f32[16,128,256]{2,1,0:T(8,128)} fusion(bf16[16,256,1024]{2,1,0:T(8,128)(2,1)} %bitcast.63, bf16[128,2048]{1,0:T(8,128)(2,1)S(1)} %bitcast.68, s32[]{:T(128)S(6)} %select_n.36), kind=kOutput, calls=%fused_computation.9 | convolution fusion | flops 1073741824 | bytes 10747908 | tf_op jit(solution)/shard_map/dot_general | solution.py:78
  102.3 7.2 %all-to-all-start.3 = ((f32[16,128,256]{2,1,0:T(8,128)}), f32[16,128,256]{2,1,0:T(8,128)S(1)}, u32[]{:S(2)}, u32[]{:S(2)}) async-start(f32[16,128,256]{2,1,0:T(8,128)} %convolution_bitcast_fusion.1), calls=%async_computation.3 | async-start | bytes 4194304 | tf_op jit(solution)/shard_map/all_to_all | solution.py:16
  109.6 28.4 %all-to-all-done.3 = f32[16,128,256]{2,1,0:T(8,128)S(1)} async-done(((f32[16,128,256]{2,1,0:T(8,128)}), f32[16,128,256]{2,1,0:T(8,128)S(1)}, u32[]{:S(2)}, u32[]{:S(2)}) %all-to-all-start.3) | async-done | bytes 2097184 | tf_op jit(solution)/shard_map/all_to_all | solution.py:16
  138.1 1.6 divide_add_fusion.1
  142.2 1.4 dynamic_update_slice.22
  143.6 3.3 all-to-all-start.6
  147.0 36.2 %all-gather.3.cloned.1.call-done = f32[128,4096]{1,0:T(8,128)} async-done(((f32[128,256]{1,0:T(8,128)}), f32[128,4096]{1,0:T(8,128)}) %all-gather.3.cloned.1.call-update) | async-done | bytes 2097168 | tf_op jit(solution)/shard_map/all_gather | solution.py:91
  183.1 7.4 %fusion = f32[128,1024]{0,1:T(8,128)S(1)} fusion(bf16[1,4096,1024]{2,1,0:T(8,128)(2,1)} %get-tuple-element.10, f32[128,4096]{1,0:T(8,128)} %all-gather.3.cloned.1.call-done), kind=kOutput, calls=%fused_computation.4 | convolution fusion | flops 1074266112 | bytes 11010048 | tf_op jit(solution)/shard_map/dot_general | solution.py:51
  191.6 3.0 dynamic_update_slice.21
  194.5 4.2 %all-to-all-start.5 = ((f32[8,128,256]{1,2,0:T(8,128)}), f32[8,128,256]{1,2,0:T(8,128)S(1)}, u32[]{:S(2)}, u32[]{:S(2)}) async-start(f32[8,128,256]{1,2,0:T(8,128)} %bitcast.19), calls=%async_computation.5 | async-start | bytes 2097152 | tf_op jit(solution)/shard_map/all_to_all | solution.py:16
  198.8 15.2 %all-to-all-done.5 = f32[8,128,256]{1,2,0:T(8,128)S(1)} async-done(((f32[8,128,256]{1,2,0:T(8,128)}), f32[8,128,256]{1,2,0:T(8,128)S(1)}, u32[]{:S(2)}, u32[]{:S(2)}) %all-to-all-start.5) | async-done | bytes 1048608 | tf_op jit(solution)/shard_map/all_to_all | solution.py:16
  214.4 18.1 %all_to_all.67 = f32[8,128,256]{2,1,0:T(8,128)S(1)} all-to-all(f32[8,128,256]{2,1,0:T(8,128)S(1)} %broadcast_in_dim.14), channel_id=1, replica_groups=mesh['slab'=8,'view'=16] {'slab'}, dimensions={0} | all-to-all | bytes 2097152 | tf_op jit(solution)/shard_map/all_to_all | solution.py:22
  232.5 6.2 %all-to-all-start.9 = ((f32[16,1,256]{2,1,0:T(1,128)}), f32[16,1,256]{2,1,0:T(1,128)S(1)}, u32[]{:S(2)}, u32[]{:S(2)}) async-start(f32[16,1,256]{2,1,0:T(1,128)} %bitcast.26), calls=%async_computation.9 | async-start | bytes 32768 | tf_op jit(solution)/shard_map/all_to_all | solution.py:16
  238.8 7.6 %convolution_bitcast_fusion = f32[16,128,256]{2,1,0:T(8,128)} fusion(bf16[16,256,1024]{2,1,0:T(8,128)(2,1)} %bitcast.62, bf16[128,2048]{1,0:T(8,128)(2,1)S(1)} %bitcast.69, s32[]{:T(128)S(6)} %select_n.38), kind=kOutput, calls=%fused_computation.8 | convolution fusion | flops 1073741824 | bytes 10747908 | tf_op jit(solution)/shard_map/dot_general | solution.py:78
  246.4 7.2 %all-to-all-start.8 = ((f32[16,128,256]{2,1,0:T(8,128)}), f32[16,128,256]{2,1,0:T(8,128)}, u32[]{:S(2)}, u32[]{:S(2)}) async-start(f32[16,128,256]{2,1,0:T(8,128)} %convolution_bitcast_fusion), calls=%async_computation.8 | async-start | bytes 4194304 | tf_op jit(solution)/shard_map/all_to_all | solution.py:16
  253.7 28.5 %all-to-all-done.8 = f32[16,128,256]{2,1,0:T(8,128)} async-done(((f32[16,128,256]{2,1,0:T(8,128)}), f32[16,128,256]{2,1,0:T(8,128)}, u32[]{:S(2)}, u32[]{:S(2)}) %all-to-all-start.8) | async-done | bytes 2097184 | tf_op jit(solution)/shard_map/all_to_all | solution.py:16
  282.2 1.7 reduce_sum.117
  283.9 1.6 divide_add_fusion
  286.2 1.6 broadcast_in_dim.28
  290.6 38.3 %all-gather.5.cloned.1.call-done = f32[128,4096]{1,0:T(8,128)} async-done(((f32[128,256]{1,0:T(8,128)}), f32[128,4096]{1,0:T(8,128)}) %all-gather.5.cloned.1.call-update) | async-done | bytes 2097168 | tf_op jit(solution)/shard_map/all_gather | solution.py:91
  328.9 3.1 copy.76
  (40 shorter events, 9.0 us)
Async XLA Ops:
  15.0 23.3 %copy-start = (f32[128,4096]{1,0:T(8,128)S(1)}, f32[128,4096]{1,0:T(8,128)}, u32[]{:S(2)}) copy-start(f32[128,4096]{1,0:T(8,128)} %param.5) | copy-start | bytes 6291460
  31.5 16.5 %all-to-all-start.1 = ((f32[8,1,256]{2,1,0:T(1,128)}), f32[8,1,256]{2,1,0:T(1,128)S(1)}, u32[]{:S(2)}, u32[]{:S(2)}) async-start(f32[8,1,256]{2,1,0:T(1,128)} %bitcast.7), calls=%async_computation.1 | async-start | bytes 16384 | tf_op jit(solution)/shard_map/all_to_all | solution.py:16
  48.0 19.1 %all-to-all-start = ((f32[8,128,256]{1,2,0:T(8,128)}), f32[8,128,256]{1,2,0:T(8,128)S(1)}, u32[]{:S(2)}, u32[]{:S(2)}) async-start(f32[8,128,256]{1,2,0:T(8,128)} %bitcast.6), calls=%async_computation | async-start | bytes 2097152 | tf_op jit(solution)/shard_map/all_to_all | solution.py:16
  85.6 16.7 %all-to-all-start.4 = ((f32[16,1,256]{2,1,0:T(1,128)}), f32[16,1,256]{2,1,0:T(1,128)S(1)}, u32[]{:S(2)}, u32[]{:S(2)}) async-start(f32[16,1,256]{2,1,0:T(1,128)} %bitcast.13), calls=%async_computation.4 | async-start | bytes 32768 | tf_op jit(solution)/shard_map/all_to_all | solution.py:16
  102.3 35.7 %all-to-all-start.3 = ((f32[16,128,256]{2,1,0:T(8,128)}), f32[16,128,256]{2,1,0:T(8,128)S(1)}, u32[]{:S(2)}, u32[]{:S(2)}) async-start(f32[16,128,256]{2,1,0:T(8,128)} %convolution_bitcast_fusion.1), calls=%async_computation.3 | async-start | bytes 4194304 | tf_op jit(solution)/shard_map/all_to_all | solution.py:16
  109.5 73.6 %all-gather.3.cloned.1.call-start = ((), (), s32[]{:S(2)}) async-start(), calls=%async_computation.10 | async-start | bytes 2228224 | tf_op jit(solution)/shard_map/all_gather | solution.py:91
  143.6 50.9 %all-to-all-start.6 = ((f32[8,1,256]{2,1,0:T(1,128)}), f32[8,1,256]{2,1,0:T(1,128)S(1)}, u32[]{:S(2)}, u32[]{:S(2)}) async-start(f32[8,1,256]{2,1,0:T(1,128)} %bitcast.20), calls=%async_computation.6 | async-start | bytes 16384 | tf_op jit(solution)/shard_map/all_to_all | solution.py:16
  194.5 19.5 %all-to-all-start.5 = ((f32[8,128,256]{1,2,0:T(8,128)}), f32[8,128,256]{1,2,0:T(8,128)S(1)}, u32[]{:S(2)}, u32[]{:S(2)}) async-start(f32[8,128,256]{1,2,0:T(8,128)} %bitcast.19), calls=%async_computation.5 | async-start | bytes 2097152 | tf_op jit(solution)/shard_map/all_to_all | solution.py:16
  232.5 13.9 %all-to-all-start.9 = ((f32[16,1,256]{2,1,0:T(1,128)}), f32[16,1,256]{2,1,0:T(1,128)S(1)}, u32[]{:S(2)}, u32[]{:S(2)}) async-start(f32[16,1,256]{2,1,0:T(1,128)} %bitcast.26), calls=%async_computation.9 | async-start | bytes 32768 | tf_op jit(solution)/shard_map/all_to_all | solution.py:16
  246.4 35.8 %all-to-all-start.8 = ((f32[16,128,256]{2,1,0:T(8,128)}), f32[16,128,256]{2,1,0:T(8,128)}, u32[]{:S(2)}, u32[]{:S(2)}) async-start(f32[16,128,256]{2,1,0:T(8,128)} %convolution_bitcast_fusion), calls=%async_computation.8 | async-start | bytes 4194304 | tf_op jit(solution)/shard_map/all_to_all | solution.py:16
  253.6 75.3 %all-gather.5.cloned.1.call-start = ((), (), s32[]{:S(2)}) async-start(), calls=%async_computation.11 | async-start | bytes 2228224 | tf_op jit(solution)/shard_map/all_gather | solution.py:91
Sparse Core Ops, SparseCore 0:
  139.9 43.2 all-gather.2
  285.7 43.1 all-gather.4
where the time goes:
time: 340 us; the launch traced here: 339 us
  waiting for transfers between devices  160 us (47%)
  starting transfers between devices  49.1 us (14%)
  blocking collectives  36.2 us (11%)
  matrix products  28.3 us (8%)
  local copies, waits for them, and re-layouts  23.5 us (7%)
  between operations  21.9 us (6%)
  other arithmetic  20.2 us (6%)
    all_to_all x8, waiting for transfers between devices, sent_and_summed(): lax.all_to_all(tiles, axis, split_axis=0, concat_axis=0, tiled=True)  85.1 us
    all_gather x2, waiting for transfers between devices, per_device(): volume = lax.all_gather(new_part, 'view', axis=1, tiled=True)  74.4 us
    all_to_all x8, starting transfers between devices, sent_and_summed(): lax.all_to_all(tiles, axis, split_axis=0, concat_axis=0, tiled=True)  49.1 us
    all_to_all x2, blocking collectives, sent_to_all(): lax.all_to_all(jnp.broadcast_to(array[None], (length, *array.shape)), axi...  36.2 us
    dot_general x2, matrix products, per_device(): lax.dot_general(band_values, footprint, (((1,), (1,)), ((), ())), preferr...  15.2 us
    reduce_sum x1, other arithmetic, per_device(): col_total = jnp.sum(footprint, axis=1, dtype=jnp.float32)  13.8 us
    dot_general x2, matrix products, per_device(): jnp.dot(volume.astype(jnp.bfloat16), footprint, preferred_element_type=jn...  13.1 us
  transfers between devices with their start and end apart: 10, of which 6 were waited for; matrix products, arithmetic and copies ran while one was open for 13% of the time, Pallas kernels for 0%

commit v1 on v0

--- a/solution.py
+++ b/solution.py
@@ -88,7 +88,10 @@
             volume, lax.axis_index("view") * share_width, share_width, 1
         )
         new_part = volume_part + RELAXATION * back_part / weight_part[None, :]
-        volume = lax.all_gather(new_part, "view", axis=1, tiled=True)
+        size = lax.axis_size("view")
+        parts = jnp.stack([new_part for _ in range(size)])
+        parts = lax.all_to_all(parts, "view", split_axis=0, concat_axis=0)
+        volume = jnp.concatenate(parts, axis=1)
     return (volume, mismatch)
 
 

time: 340 us -> 316 us (0.929)
  waiting for transfers between devices: 160 us -> 131 us
  between operations: 21.9 us -> 8.53 us
  starting transfers between devices: 49.1 us -> 58.5 us
  local copies, waits for them, and re-layouts: 23.5 us -> 31.4 us
    all_gather x2 -> x0, waiting for transfers between devices: 74.4 us -> none  [per_device(): volume = lax.all_gather(new_part, 'view', axis=1, tiled=True)]
    all_to_all x0 -> x2, waiting for transfers between devices: none -> 48.3 us  [per_device(): parts = lax.all_to_all(parts, 'view', split_axis=0, concat_axis=0)]
    all_to_all x0 -> x2, starting transfers between devices: none -> 9.52 us  [per_device(): parts = lax.all_to_all(parts, 'view', split_axis=0, concat_axis=0)]
    all_to_all x0 -> x2, local copies, waits for them, and re-layouts: none -> 3.82 us  [per_device(): parts = lax.all_to_all(parts, 'view', split_axis=0, concat_axis=0)]
  transfers between devices with their start and end apart: 10 -> 10, of which waited for: 6 -> 6; matrix products, arithmetic and copies ran while one was open for 13% -> 15% of each run, Pallas kernels for 0% -> 0%
where the time goes in v1:
time: 316 us; the launch traced here: 314 us
  waiting for transfers between devices  131 us (41%)
  starting transfers between devices  58.5 us (19%)
  blocking collectives  37.1 us (12%)
  local copies, waits for them, and re-layouts  31.4 us (10%)
  matrix products  29.1 us (9%)
  other arithmetic  18.1 us (6%)
  between operations  8.53 us (3%)
    all_to_all x8, waiting for transfers between devices, sent_and_summed(): lax.all_to_all(tiles, axis, split_axis=0, concat_axis=0, tiled=True)  83.1 us
    all_to_all x8, starting transfers between devices, sent_and_summed(): lax.all_to_all(tiles, axis, split_axis=0, concat_axis=0, tiled=True)  49 us
    all_to_all x2, waiting for transfers between devices, per_device(): parts = lax.all_to_all(parts, 'view', split_axis=0, concat_axis=0)  48.3 us
    all_to_all x2, blocking collectives, sent_to_all(): lax.all_to_all(jnp.broadcast_to(array[None], (length, *array.shape)), axi...  37.1 us
    dot_general x2, matrix products, per_device(): lax.dot_general(band_values, footprint, (((1,), (1,)), ((), ())), preferr...  15.2 us
    dot_general x2, matrix products, per_device(): jnp.dot(volume.astype(jnp.bfloat16), footprint, preferred_element_type=jn...  13.9 us
    reduce_sum x1, other arithmetic, per_device(): col_total = jnp.sum(footprint, axis=1, dtype=jnp.float32)  13.8 us
    all_to_all x2, starting transfers between devices, per_device(): parts = lax.all_to_all(parts, 'view', split_axis=0, concat_axis=0)  9.52 us
  transfers between devices with their start and end apart: 10, of which 6 were waited for; matrix products, arithmetic and copies ran while one was open for 15% of the time, Pallas kernels for 0%

profile of v1, /device:TPU:1, one launch (start us, length us, event | category | flops | bytes accessed | tf_op | source)
XLA Modules:
  0.0 314.1 jit_solution(7474503060446154873)
XLA Ops:
  8.5 13.8 %convert_reduce_fusion = (f32[4096]{0:T(1024)}, f32[1024]{0:T(1024)S(1)}, bf16[1,4096,1024]{2,1,0:T(8,128)(2,1)}, f32[1024]{0:T(1024)S(1)}, f32[4096]{0:T(1024)}, /*index=5*/bf16[1,4096,1024]{2,1,0:T(8,128)(2,1)}) fusion(bf16[2,4096,1024]{2,1,0:T(8,128)(2,1)} %param.7, s32[]{:T(128)S(6)} %select_n.37, s32[]{:T(128)S(6)} %select_n.34), kind=kLoop, calls=%fused_computation | loop fusion | flops 25155584 | bytes 33595400 | tf_op jit(solution)/shard_map/reduce_sum | solution.py:81
  24.9 6.8 %all-to-all-start.1 = ((f32[8,1,256]{2,1,0:T(1,128)}), f32[8,1,256]{2,1,0:T(1,128)S(1)}, u32[]{:S(2)}, u32[]{:S(2)}) async-start(f32[8,1,256]{2,1,0:T(1,128)} %bitcast.7), calls=%async_computation.1 | async-start | bytes 16384 | tf_op jit(solution)/shard_map/all_to_all | solution.py:16
  31.7 5.7 %fusion.4 = f32[128,1024]{0,1:T(8,128)S(1)} fusion(bf16[1,4096,1024]{2,1,0:T(8,128)(2,1)} %get-tuple-element.18, f32[128,4096]{1,0:T(8,128)S(1)} %copy-done.2), kind=kOutput, calls=%fused_computation.11 | convolution fusion | flops 1074266112 | bytes 11010048 | tf_op jit(solution)/shard_map/dot_general | solution.py:51
  38.5 3.0 dynamic_update_slice.19
  41.5 5.1 %all-to-all-start = ((f32[8,128,256]{1,2,0:T(8,128)}), f32[8,128,256]{1,2,0:T(8,128)S(1)}, u32[]{:S(2)}, u32[]{:S(2)}) async-start(f32[8,128,256]{1,2,0:T(8,128)} %bitcast.6), calls=%async_computation | async-start | bytes 2097152 | tf_op jit(solution)/shard_map/all_to_all | solution.py:16
  47.6 13.0 %all-to-all-done = f32[8,128,256]{1,2,0:T(8,128)S(1)} async-done(((f32[8,128,256]{1,2,0:T(8,128)}), f32[8,128,256]{1,2,0:T(8,128)S(1)}, u32[]{:S(2)}, u32[]{:S(2)}) %all-to-all-start) | async-done | bytes 1048608 | tf_op jit(solution)/shard_map/all_to_all | solution.py:16
  60.9 18.1 %all_to_all.76 = f32[8,128,256]{2,1,0:T(8,128)S(1)} all-to-all(f32[8,128,256]{2,1,0:T(8,128)S(1)} %broadcast_in_dim.13), channel_id=1, replica_groups=mesh['slab'=8,'view'=16] {'slab'}, dimensions={0} | all-to-all | bytes 2097152 | tf_op jit(solution)/shard_map/all_to_all | solution.py:22
  79.1 9.1 %all-to-all-start.4 = ((f32[16,1,256]{2,1,0:T(1,128)}), f32[16,1,256]{2,1,0:T(1,128)S(1)}, u32[]{:S(2)}, u32[]{:S(2)}) async-start(f32[16,1,256]{2,1,0:T(1,128)} %bitcast.13), calls=%async_computation.4 | async-start | bytes 32768 | tf_op jit(solution)/shard_map/all_to_all | solution.py:16
  88.2 7.6 %convolution_bitcast_fusion.1 = f32[16,128,256]{2,1,0:T(8,128)} fusion(bf16[16,256,1024]{2,1,0:T(8,128)(2,1)} %bitcast.72, bf16[128,2048]{1,0:T(8,128)(2,1)S(1)} %bitcast.81, s32[]{:T(128)S(6)} %select_n.36), kind=kOutput, calls=%fused_computation.10 | convolution fusion | flops 1073741824 | bytes 10747908 | tf_op jit(solution)/shard_map/dot_general | solution.py:78
  95.8 7.2 %all-to-all-start.3 = ((f32[16,128,256]{2,1,0:T(8,128)}), f32[16,128,256]{2,1,0:T(8,128)S(1)}, u32[]{:S(2)}, u32[]{:S(2)}) async-start(f32[16,128,256]{2,1,0:T(8,128)} %convolution_bitcast_fusion.1), calls=%async_computation.3 | async-start | bytes 4194304 | tf_op jit(solution)/shard_map/all_to_all | solution.py:16
  103.0 28.4 %all-to-all-done.3 = f32[16,128,256]{2,1,0:T(8,128)S(1)} async-done(((f32[16,128,256]{2,1,0:T(8,128)}), f32[16,128,256]{2,1,0:T(8,128)S(1)}, u32[]{:S(2)}, u32[]{:S(2)}) %all-to-all-start.3) | async-done | bytes 2097184 | tf_op jit(solution)/shard_map/all_to_all | solution.py:16
  132.5 1.5 stack.4
  134.1 4.4 %all-to-all-start.5 = ((f32[16,128,256]{2,1,0:T(8,128)}), f32[16,128,256]{2,1,0:T(8,128)S(1)}, u32[]{:S(2)}, u32[]{:S(2)}) async-start(f32[16,128,256]{2,1,0:T(8,128)} %stack.4), calls=%async_computation.5 | async-start | bytes 4194304 | tf_op jit(solution)/shard_map/all_to_all | solution.py:93
  142.3 24.7 %all-to-all-done.5 = f32[16,128,256]{2,1,0:T(8,128)S(1)} async-done(((f32[16,128,256]{2,1,0:T(8,128)}), f32[16,128,256]{2,1,0:T(8,128)S(1)}, u32[]{:S(2)}, u32[]{:S(2)}) %all-to-all-start.5) | async-done | bytes 2097184 | tf_op jit(solution)/shard_map/all_to_all | solution.py:93
  168.4 3.5 %all-to-all-start.7 = ((f32[8,1,256]{2,1,0:T(1,128)}), f32[8,1,256]{2,1,0:T(1,128)S(1)}, u32[]{:S(2)}, u32[]{:S(2)}) async-start(f32[8,1,256]{2,1,0:T(1,128)} %bitcast.23), calls=%async_computation.7 | async-start | bytes 16384 | tf_op jit(solution)/shard_map/all_to_all | solution.py:16
  171.9 1.9 copy.68
  174.0 8.2 %fusion = f32[128,1024]{0,1:T(8,128)} fusion(bf16[128,4096]{0,1:T(8,128)(2,1)S(1)} %bitcast.77, bf16[1,4096,1024]{2,1,0:T(8,128)(2,1)} %get-tuple-element.14), kind=kOutput, calls=%fused_computation.4 | convolution fusion | flops 1073741824 | bytes 9961472 | tf_op jit(solution)/shard_map/dot_general | solution.py:51
  183.2 3.0 dynamic_update_slice.21
  186.2 4.9 %all-to-all-start.6 = ((f32[8,128,256]{1,2,0:T(8,128)}), f32[8,128,256]{1,2,0:T(8,128)S(1)}, u32[]{:S(2)}, u32[]{:S(2)}) async-start(f32[8,128,256]{1,2,0:T(8,128)} %bitcast.78), calls=%async_computation.6 | async-start | bytes 2097152 | tf_op jit(solution)/shard_map/all_to_all | solution.py:16
  191.2 14.1 %all-to-all-done.6 = f32[8,128,256]{1,2,0:T(8,128)S(1)} async-done(((f32[8,128,256]{1,2,0:T(8,128)}), f32[8,128,256]{1,2,0:T(8,128)S(1)}, u32[]{:S(2)}, u32[]{:S(2)}) %all-to-all-start.6) | async-done | bytes 1048608 | tf_op jit(solution)/shard_map/all_to_all | solution.py:16
  205.7 18.9 %all_to_all.77 = f32[8,128,256]{2,1,0:T(8,128)S(1)} all-to-all(f32[8,128,256]{2,1,0:T(8,128)S(1)} %broadcast_in_dim.14), channel_id=1, replica_groups=mesh['slab'=8,'view'=16] {'slab'}, dimensions={0} | all-to-all | bytes 2097152 | tf_op jit(solution)/shard_map/all_to_all | solution.py:22
  224.6 5.2 %all-to-all-start.10 = ((f32[16,1,256]{2,1,0:T(1,128)}), f32[16,1,256]{2,1,0:T(1,128)S(1)}, u32[]{:S(2)}, u32[]{:S(2)}) async-start(f32[16,1,256]{2,1,0:T(1,128)} %bitcast.29), calls=%async_computation.10 | async-start | bytes 32768 | tf_op jit(solution)/shard_map/all_to_all | solution.py:16
  229.9 7.6 %convolution_bitcast_fusion = f32[16,128,256]{2,1,0:T(8,128)} fusion(bf16[16,256,1024]{2,1,0:T(8,128)(2,1)} %bitcast.71, bf16[128,2048]{1,0:T(8,128)(2,1)S(1)} %bitcast.82, s32[]{:T(128)S(6)} %select_n.38), kind=kOutput, calls=%fused_computation.9 | convolution fusion | flops 1073741824 | bytes 10747908 | tf_op jit(solution)/shard_map/dot_general | solution.py:78
  237.5 7.2 %all-to-all-start.9 = ((f32[16,128,256]{2,1,0:T(8,128)}), f32[16,128,256]{2,1,0:T(8,128)}, u32[]{:S(2)}, u32[]{:S(2)}) async-start(f32[16,128,256]{2,1,0:T(8,128)} %convolution_bitcast_fusion), calls=%async_computation.9 | async-start | bytes 4194304 | tf_op jit(solution)/shard_map/all_to_all | solution.py:16
  245.8 27.5 %all-to-all-done.9 = f32[16,128,256]{2,1,0:T(8,128)} async-done(((f32[16,128,256]{2,1,0:T(8,128)}), f32[16,128,256]{2,1,0:T(8,128)}, u32[]{:S(2)}, u32[]{:S(2)}) %all-to-all-start.9) | async-done | bytes 2097184 | tf_op jit(solution)/shard_map/all_to_all | solution.py:16
  273.4 1.7 reduce_sum.117
  275.1 1.5 stack.5
  276.6 5.1 %all-to-all-start.11 = ((f32[16,128,256]{2,1,0:T(8,128)}), f32[16,128,256]{2,1,0:T(8,128)}, u32[]{:S(2)}, u32[]{:S(2)}) async-start(f32[16,128,256]{2,1,0:T(8,128)} %stack.5), calls=%async_computation.11 | async-start | bytes 4194304 | tf_op jit(solution)/shard_map/all_to_all | solution.py:93
  282.4 1.6 broadcast_in_dim.28
  286.8 23.6 %all-to-all-done.11 = f32[16,128,256]{2,1,0:T(8,128)} async-done(((f32[16,128,256]{2,1,0:T(8,128)}), f32[16,128,256]{2,1,0:T(8,128)}, u32[]{:S(2)}, u32[]{:S(2)}) %all-to-all-start.11) | async-done | bytes 2097184 | tf_op jit(solution)/shard_map/all_to_all | solution.py:93
  310.4 1.9 copy.77
  312.3 1.8 copy.80
  (49 shorter events, 17.9 us)
Async XLA Ops:
  8.5 23.2 %copy-start.2 = (f32[128,4096]{1,0:T(8,128)S(1)}, f32[128,4096]{1,0:T(8,128)}, u32[]{:S(2)}) copy-start(f32[128,4096]{1,0:T(8,128)} %param.5) | copy-start | bytes 6291460
  24.9 16.5 %all-to-all-start.1 = ((f32[8,1,256]{2,1,0:T(1,128)}), f32[8,1,256]{2,1,0:T(1,128)S(1)}, u32[]{:S(2)}, u32[]{:S(2)}) async-start(f32[8,1,256]{2,1,0:T(1,128)} %bitcast.7), calls=%async_computation.1 | async-start | bytes 16384 | tf_op jit(solution)/shard_map/all_to_all | solution.py:16
  41.5 19.1 %all-to-all-start = ((f32[8,128,256]{1,2,0:T(8,128)}), f32[8,128,256]{1,2,0:T(8,128)S(1)}, u32[]{:S(2)}, u32[]{:S(2)}) async-start(f32[8,128,256]{1,2,0:T(8,128)} %bitcast.6), calls=%async_computation | async-start | bytes 2097152 | tf_op jit(solution)/shard_map/all_to_all | solution.py:16
  79.1 16.7 %all-to-all-start.4 = ((f32[16,1,256]{2,1,0:T(1,128)}), f32[16,1,256]{2,1,0:T(1,128)S(1)}, u32[]{:S(2)}, u32[]{:S(2)}) async-start(f32[16,1,256]{2,1,0:T(1,128)} %bitcast.13), calls=%async_computation.4 | async-start | bytes 32768 | tf_op jit(solution)/shard_map/all_to_all | solution.py:16
  95.8 35.7 %all-to-all-start.3 = ((f32[16,128,256]{2,1,0:T(8,128)}), f32[16,128,256]{2,1,0:T(8,128)S(1)}, u32[]{:S(2)}, u32[]{:S(2)}) async-start(f32[16,128,256]{2,1,0:T(8,128)} %convolution_bitcast_fusion.1), calls=%async_computation.3 | async-start | bytes 4194304 | tf_op jit(solution)/shard_map/all_to_all | solution.py:16
  134.1 33.0 %all-to-all-start.5 = ((f32[16,128,256]{2,1,0:T(8,128)}), f32[16,128,256]{2,1,0:T(8,128)S(1)}, u32[]{:S(2)}, u32[]{:S(2)}) async-start(f32[16,128,256]{2,1,0:T(8,128)} %stack.4), calls=%async_computation.5 | async-start | bytes 4194304 | tf_op jit(solution)/shard_map/all_to_all | solution.py:93
  167.1 1.3 copy-start.1
  168.4 17.8 %all-to-all-start.7 = ((f32[8,1,256]{2,1,0:T(1,128)}), f32[8,1,256]{2,1,0:T(1,128)S(1)}, u32[]{:S(2)}, u32[]{:S(2)}) async-start(f32[8,1,256]{2,1,0:T(1,128)} %bitcast.23), calls=%async_computation.7 | async-start | bytes 16384 | tf_op jit(solution)/shard_map/all_to_all | solution.py:16
  173.8 8.4 %copy-start = (f32[16,128,256]{1,2,0:T(8,128)}, f32[16,128,256]{1,2,0:T(8,128)S(1)}, u32[]{:S(2)}) copy-start(f32[16,128,256]{1,2,0:T(8,128)S(1)} %copy.68) | copy-start | bytes 6291460
  186.2 19.1 %all-to-all-start.6 = ((f32[8,128,256]{1,2,0:T(8,128)}), f32[8,128,256]{1,2,0:T(8,128)S(1)}, u32[]{:S(2)}, u32[]{:S(2)}) async-start(f32[8,128,256]{1,2,0:T(8,128)} %bitcast.78), calls=%async_computation.6 | async-start | bytes 2097152 | tf_op jit(solution)/shard_map/all_to_all | solution.py:16
  224.6 12.9 %all-to-all-start.10 = ((f32[16,1,256]{2,1,0:T(1,128)}), f32[16,1,256]{2,1,0:T(1,128)S(1)}, u32[]{:S(2)}, u32[]{:S(2)}) async-start(f32[16,1,256]{2,1,0:T(1,128)} %bitcast.29), calls=%async_computation.10 | async-start | bytes 32768 | tf_op jit(solution)/shard_map/all_to_all | solution.py:16
  237.5 35.8 %all-to-all-start.9 = ((f32[16,128,256]{2,1,0:T(8,128)}), f32[16,128,256]{2,1,0:T(8,128)}, u32[]{:S(2)}, u32[]{:S(2)}) async-start(f32[16,128,256]{2,1,0:T(8,128)} %convolution_bitcast_fusion), calls=%async_computation.9 | async-start | bytes 4194304 | tf_op jit(solution)/shard_map/all_to_all | solution.py:16
  276.6 33.7 %all-to-all-start.11 = ((f32[16,128,256]{2,1,0:T(8,128)}), f32[16,128,256]{2,1,0:T(8,128)}, u32[]{:S(2)}, u32[]{:S(2)}) async-start(f32[16,128,256]{2,1,0:T(8,128)} %stack.5), calls=%async_computation.11 | async-start | bytes 4194304 | tf_op jit(solution)/shard_map/all_to_all | solution.py:93
